TPU v7x, 32 devices: a whole 2x2x4 slice. The times are simulated.
32 devices in a mesh: aa: 8 (over y, x, core), ba: 4 (over z).
Axes of the slice: x: 2, y: 2, z: 4, core: 2. Of those that a mesh axis runs over, the one named last changes fastest.
Arguments:
- cotangent: bfloat16 [1, 20, 64, 64, 2048], P(None, None, 'aa', 'ba'), may hold values from -6 to 6
- pre_activations: bfloat16 [2, 1, 20, 64, 64, 2048], P(None, None, None, 'aa', 'ba'), may hold values from -6 to 6
- spectral_weights: bfloat16 [2, 2, 20, 20, 24, 6912], P(None, None, None, None, 'ba', 'aa'), may hold values from -6 to 6
- skip_weights: bfloat16 [2, 20, 20], replicated, may hold values from -1.25 to 1.25
- lift_weights: float32 [20], replicated, may hold values from -1.25 to 1.25
Outputs:
- perm_grad: float32 [1, 64, 64, 2048], P(None, 'aa', 'ba')
All inputs are finite; a program needn't handle non-finite values.
Results may differ from a plain program's by a relative error of at most 0.023.
Values may be sent and summed in bfloat16 or wider, within the bound.
A program may use at most 256 MiB of HBM per device.

v0:
```python
import math

import jax
import jax.numpy as jnp
from jax import lax
from jax.sharding import PartitionSpec as P

NX = 64
NY = 64
NZ = 64
NT = 32
KX = 24
KY = 24
KZ = 24
KT = 12


def gelu_slope(values):
    normal_cdf = 0.5 * (1.0 + lax.erf(values / math.sqrt(2.0)))
    density = jnp.exp(-0.5 * values * values) / math.sqrt(2.0 * math.pi)
    return normal_cdf + values * density


def signed_freq(total_count):
    index_list = jnp.arange(total_count, dtype=jnp.int32)
    return jnp.where(index_list < total_count // 2, index_list, index_list - total_count)


def line_tables(total_count, length):
    places = jnp.arange(length, dtype=jnp.int32)
    whole_turns = signed_freq(total_count)[:, None] * places[None, :] % length
    angles = 2.0 * math.pi / length * whole_turns.astype(jnp.float32)
    cosine = jnp.cos(angles)
    sine_part = jnp.sin(angles)
    forward = jnp.stack(
        [jnp.stack([cosine.T, -sine_part.T], 1), jnp.stack([sine_part.T, cosine.T], 1)], 0
    )
    inverse = (
        jnp.stack([jnp.stack([cosine, sine_part], 1), jnp.stack([-sine_part, cosine], 1)], 0)
        / length
    )
    return (forward, inverse)


def plane_tables():
    joint_index = jnp.arange(KZ * KT, dtype=jnp.int32)
    depth_freq = signed_freq(KZ)[joint_index // KT]
    time_freq = joint_index % KT
    cell_index = jnp.arange(NZ * NT, dtype=jnp.int32)
    depth_place = cell_index // NT
    time_place = cell_index % NT
    whole_turns = (
        depth_freq[:, None] * depth_place[None, :] * NT
        + time_freq[:, None] * time_place[None, :] * NZ
    ) % (NZ * NT)
    angles = 2.0 * math.pi / (NZ * NT) * whole_turns.astype(jnp.float32)
    forward = jnp.stack([jnp.cos(angles).T, -jnp.sin(angles).T], 1)
    inverse = jnp.stack([jnp.cos(angles), -jnp.sin(angles)], 0) / (NZ * NT)
    return (forward, inverse)


def halves(matrix):
    coarse = matrix.astype(jnp.bfloat16)
    remainder = (matrix - coarse.astype(jnp.float32)).astype(jnp.bfloat16)
    return (coarse, remainder)


def split_product(pattern, values, halves_pair):
    first = jnp.einsum(pattern, values, halves_pair[0], preferred_element_type=jnp.float32)
    return first + jnp.einsum(pattern, values, halves_pair[1], preferred_element_type=jnp.float32)


def exact_product(pattern, values, matrix):
    return jnp.einsum(pattern, values, matrix, precision=lax.Precision.HIGHEST)


def reshaped(tables, shape):
    return jax.tree.map(lambda table: table.reshape(shape), tables)


def to_bf16(values):
    return values.astype(jnp.bfloat16)


def keep_float(values):
    return values


def forward_modes(grad_pre, weights, forward_pairs):
    plane_pair, first_pair, second_pair = forward_pairs
    plane_spectrum = split_product("bcxyz,zpm->bcpxmy", grad_pre, plane_pair)
    extent = plane_spectrum.shape
    plane_spectrum = plane_spectrum.reshape(
        extent[0], extent[1], 2, extent[3], extent[4] * extent[5]
    ).astype(jnp.bfloat16)
    first_spectrum = split_product(
        "bcpxr,pxqk->bcqkr",
        lax.all_to_all(plane_spectrum, "aa", split_axis=4, concat_axis=3, tiled=True),
        first_pair,
    ).astype(jnp.bfloat16)
    blocks = lax.all_to_all(first_spectrum, "ba", split_axis=3, concat_axis=4, tiled=True)
    shape_now = blocks.shape
    column_count = lax.axis_size("ba")
    local_rows = NY // column_count
    local_modes = shape_now[4] // NY
    values = blocks.reshape(
        shape_now[0], shape_now[1], 2, shape_now[3], column_count, local_modes, local_rows
    )
    table = reshaped(second_pair, (2, column_count, local_rows, 2, KY))
    result = split_product("bcpksmu,psuqj->bcqkmj", values, table)
    spectrum = result.reshape(shape_now[0], shape_now[1], 2, shape_now[3], local_modes * KY).astype(
        jnp.bfloat16
    )
    real_part = spectrum[:, :, 0]
    imag_part = spectrum[:, :, 1]

    def mixing(values, matrix):
        return jnp.einsum("bokr,oikr->bikr", values, matrix, preferred_element_type=jnp.float32)

    result_real = mixing(real_part, weights[0]) + mixing(imag_part, weights[1])
    result_imag = mixing(imag_part, weights[0]) - mixing(real_part, weights[1])
    return jnp.stack([result_real, result_imag], 2)


def back_path(mode_values, tables, multiply, finish, first_move, second_move):
    first_table, second_table, plane_table = tables
    extent = mode_values.shape
    local_modes = extent[4] // KY
    gridded = mode_values.reshape(extent[0], extent[1], 2, extent[3], local_modes, KY)
    back_second = multiply("bcpkmj,pjqy->bcqkym", gridded, second_table)
    back_second = finish(back_second.reshape(extent[0], extent[1], 2, extent[3], NY * local_modes))

    def back_first_axis(blocks):
        return finish(multiply("bcpkr,pkqx->bcqxr", blocks, first_table))

    back_first = first_move(back_second, back_first_axis)

    def plane_axes(blocks):
        shape_now = blocks.shape
        row_count = lax.axis_size("aa")
        mode_share = KZ * KT // row_count
        local_rows = shape_now[4] // (KZ * KT)
        values = blocks.reshape(
            shape_now[0], shape_now[1], 2, shape_now[3], row_count, local_rows, mode_share
        )
        table = reshaped(plane_table, (2, row_count, mode_share, NZ * NT))
        return multiply("bcpxsyn,psnz->bcxyz", values, table)

    return second_move(back_first, plane_axes)


def per_device(cotangent, pre_activations, spectral_weights, skip_weights, lift_weights):
    plane_forward, plane_inverse = plane_tables()
    first_forward, first_inverse = line_tables(KX, NX)
    second_forward, second_inverse = line_tables(KY, NY)
    forward_pairs = (halves(plane_forward), halves(first_forward), halves(second_forward))
    back_pairs = (halves(first_inverse), halves(second_inverse), halves(plane_inverse))
    exact_tables = (first_inverse, second_inverse, plane_inverse)
    incoming = cotangent.astype(jnp.float32)
    layers = pre_activations.shape[0]
    perm_grad = None
    for layer_index in range(layers - 1, -1, -1):
        slope = gelu_slope(pre_activations[layer_index].astype(jnp.float32))
        grad_pre = (incoming * slope).astype(jnp.bfloat16)
        mode_values = forward_modes(grad_pre, spectral_weights[layer_index], forward_pairs)
        skip_term = jnp.einsum(
            "boxyz,oi->bixyz",
            grad_pre,
            skip_weights[layer_index],
            preferred_element_type=jnp.float32,
        )
        if layer_index > 0:
            spectral = back_path(
                mode_values.astype(jnp.bfloat16),
                back_pairs,
                split_product,
                to_bf16,
                lambda values, worker: worker(
                    lax.all_to_all(values, "ba", split_axis=4, concat_axis=3, tiled=True)
                ),
                lambda values, worker: worker(
                    lax.all_to_all(values, "aa", split_axis=3, concat_axis=4, tiled=True)
                ),
            )
            incoming = skip_term + spectral
        else:
            folded = jnp.einsum(
                "bcpkr,c->bpkr", mode_values, lift_weights, precision=lax.Precision.HIGHEST
            )[:, None]
            spectral = back_path(
                folded,
                exact_tables,
                exact_product,
                keep_float,
                lambda values, worker: worker(
                    lax.all_to_all(values, "ba", split_axis=4, concat_axis=3, tiled=True)
                ),
                lambda values, worker: worker(
                    lax.all_to_all(
                        values.astype(jnp.bfloat16), "aa", split_axis=3, concat_axis=4, tiled=True
                    ).astype(values.dtype)
                ),
            )
            projected = jnp.einsum(
                "bcxyz,c->bxyz", skip_term, lift_weights, precision=lax.Precision.HIGHEST
            )
            perm_grad = projected + spectral[:, 0]
    return perm_grad


def solution(mesh):
    return jax.shard_map(
        per_device,
        mesh=mesh,
        in_specs=(
            P(None, None, "aa", "ba", None),
            P(None, None, None, "aa", "ba", None),
            P(None, None, None, None, "ba", "aa"),
            P(),
            P(),
        ),
        out_specs=P(None, "aa", "ba", None),
        check_vma=False,
    )
```

profile of v0, /device:TPU:0, one launch (start us, length us, event | category | flops | bytes accessed | tf_op | source)
XLA Modules:
  0.0 969.6 jit_solution(8584640698569126832)
XLA Ops:
  2.1 11.6 %fusion.37 = bf16[20,8,16,2048]{3,2,1,0:T(8,128)(2,1)S(1)} fusion(bf16[2,1,20,8,16,2048]{5,4,3,2,1,0:T(8,128)(2,1)} %param.6, bf16[1,20,8,16,2048]{4,3,2,1,0:T(8,128)(2,1)} %param.5), kind=kLoop, calls=%fused_computation.53 | loop fusion | flops 62914560 | bytes 31457280 | tf_op jit(solution)/shard_map/reshape
  13.7 4.6 fusion.202
  18.3 10.7 %select_select_fusion = s32[288]{0:T(512)S(1)} fusion(pred[288]{0:T(512)(128)(4,1)S(1)} %compare_reduce_fusion, pred[288]{0:T(512)(128)(4,1)S(1)} %compare_reduce_fusion.1, pred[288]{0:T(512)(128)(4,1)S(1)} %compare_reduce_fusion.2, pred[288]{0:T(512)(128)(4,1)S(1)} %compare_reduce_fusion.3, pred[288]{0:T(512)(128)(4,1)S(1)} %compare_reduce_fusion.4, ...), kind=kLoop, calls=%fused_computation.276 | loop fusion | flops 4896 | bytes 7268 | tf_op jit(solution)/shard_map/gather | solution.py:47
  29.1 9.7 fusion.130
  38.8 16.4 %fusion.23 = f32[2,288,20,8,16]{1,2,4,3,0:T(8,128)} fusion(bf16[20,8,16,2048]{3,2,1,0:T(8,128)(2,1)S(1)} %fusion.37, f32[2048,1,288]{0,2,1:T(8,128)S(1)} %get-tuple-element.30, f32[2048,1,288]{0,2,1:T(8,128)S(1)} %get-tuple-element.29), kind=kOutput, calls=%fused_computation.41 | convolution fusion | flops 6045696000 | bytes 21102592 | tf_op jit(solution)/shard_map/bcxyz,zpm->bcpxmy/dot_general | solution.py:70
  55.1 22.8 %fusion.58 = bf16[1,20,2,8,288,16]{4,1,5,3,2,0:T(8,128)(2,1)} fusion(f32[2,288,20,8,16]{1,2,4,3,0:T(8,128)} %fusion.23, bf16[20,8,16,2048]{3,2,1,0:T(8,128)(2,1)} %copy-done.3, f32[2048,1,288]{0,2,1:T(8,128)S(1)} %get-tuple-element.30, f32[2048,1,288]{0,2,1:T(8,128)S(1)} %get-tuple-element.29), kind=kOutput, calls=%fused_computation.84 | convolution fusion | flops 6047465472 | bytes 24051712 | tf_op jit(solution)/shard_map/bcxyz,zpm->bcpxmy/dot_general | solution.py:69
  78.0 20.4 %copy.371 = bf16[1,20,2,8,288,16]{1,3,2,5,4,0:T(8,128)(2,1)} copy(bf16[1,20,2,8,288,16]{4,1,5,3,2,0:T(8,128)(2,1)} %fusion.58) | data formatting | bytes 5898240 | tf_op jit(solution)/shard_map/convert_element_type | solution.py:95
  98.4 43.6 %reshape.1309 = bf16[8,2,92160]{2,1,0:T(2,128)(2,1)} reshape(bf16[4608,1,2,8,20]{4,3,2,1,0:T(8,128)(2,1)} %bitcast.538) | data formatting | bytes 5898240
  142.0 5.4 all-to-all-start
  147.6 35.5 %all-to-all-done = bf16[8,2,92160]{2,1,0:T(2,128)(2,1)S(1)} async-done(((bf16[8,2,92160]{2,1,0:T(2,128)(2,1)}), bf16[8,2,92160]{2,1,0:T(2,128)(2,1)S(1)}, u32[]{:S(2)}, u32[]{:S(2)}) %all-to-all-start) | async-done | bytes 2949152 | tf_op jit(solution)/shard_map/all_to_all | solution.py:98
  183.2 50.4 %reshape.1310 = bf16[4608,1,2,8,20]{4,3,2,1,0:T(8,128)(2,1)} reshape(bf16[8,2,92160]{2,1,0:T(2,128)(2,1)S(1)} %all-to-all-done) | data formatting | bytes 5898240
  233.6 18.8 %copy.372 = bf16[1,20,2,8,8,576]{5,4,3,2,1,0:T(8,128)(2,1)S(1)} copy(bf16[1,20,2,8,8,576]{1,3,2,5,4,0:T(8,128)(2,1)} %bitcast.540) | data formatting | bytes 5898240 | tf_op jit(solution)/shard_map/all_to_all | solution.py:98
  255.7 5.3 all-to-all-start.1
  261.0 35.0 %fusion.234 = (bf16[1,1,20,20,6,864]{5,1,4,3,2,0:T(2,128)(2,1)}, bf16[1,1,20,20,6,864]{5,1,4,3,2,0:T(2,128)(2,1)}, bf16[1,1,20,20,6,864]{5,1,4,3,2,0:T(2,128)(2,1)}, bf16[1,1,20,20,6,864]{5,1,4,3,2,0:T(2,128)(2,1)}) fusion(bf16[2,2,20,20,6,864]{5,1,4,3,2,0:T(2,128)(2,1)} %param.7), kind=kLoop, calls=%fused_computation.306 | loop fusion | bytes 33177600 | tf_op jit(solution)/shard_map/slice | solution.py:120
  297.8 8.8 reshape.1115
  306.6 10.3 %fusion.50 = f32[2,24,20,6,36,1,1]{4,1,6,3,5,2,0:T(8,128)S(1)} fusion(bf16[20,2,6,4,36,16]{5,4,3,2,1,0:T(8,128)(2,1)} %reshape.1115, f32[1,4,16,1,24]{4,2,1,0,3:T(8,128)S(1)} %get-tuple-element.39, f32[1,4,16,1,24]{4,2,1,0,3:T(8,128)S(1)} %get-tuple-element.38, f32[1,4,16,1,24]{4,2,1,0,3:T(8,128)S(1)} %get-tuple-element.37), kind=kOutput, calls=%fused_computation.66 | convolution fusion | flops 53133312 | bytes 1953792 | tf_op jit(solution)/shard_map/bcpksmu,psuqj->bcqkmj/dot_general | solution.py:69
  316.9 7.7 fusion.114
  324.6 3.2 copy.229
  327.9 3.0 convert_element_type.356
  331.8 13.7 %fusion.38 = (f32[6,864,20]{1,2,0:T(8,128)S(1)}, f32[6,864,20]{1,2,0:T(8,128)S(1)}, f32[6,864,20]{1,2,0:T(8,128)S(1)}, f32[6,864,20]{1,2,0:T(8,128)S(1)}) fusion(f32[6,864,20]{1,0,2:T(8,128)S(1)} %copy.411, bf16[1,1,20,20,6,864]{5,1,4,3,2,0:T(2,128)(2,1)} %get-tuple-element.20, f32[6,864,20]{1,0,2:T(8,128)S(1)} %copy.412, ...), kind=kLoop, calls=%fused_computation.54 | loop fusion | flops 20321280 | bytes 10782720 | tf_op jit(solution)/shard_map/bokr,oikr->bikr/dot_general | solution.py:118
  351.2 2.0 fusion.89
  353.2 15.7 %copy.381 = bf16[1,20,2,6,64,36]{1,2,3,5,4,0:T(2,128)(2,1)} copy(bf16[1,20,2,6,64,36]{4,5,3,1,2,0:T(8,128)(2,1)S(1)} %fusion.89) | data formatting | bytes 2211840 | tf_op jit(solution)/shard_map/convert_element_type | solution.py:82
  368.9 16.9 %reshape.1311 = bf16[4,2,69120]{2,1,0:T(2,128)(2,1)} reshape(bf16[2304,1,6,2,20]{4,3,2,1,0:T(2,128)(2,1)} %bitcast.546) | data formatting | bytes 2211840
  385.8 5.5 all-to-all-start.2
  391.3 10.1 %slice.56 = bf16[1,1,20,8,16,2048]{5,4,3,2,1,0:T(8,128)(2,1)} slice(bf16[2,1,20,8,16,2048]{5,4,3,2,1,0:T(8,128)(2,1)} %param.6), slice={[0:1], [0:1], [0:20], [0:8], [0:16], [0:2048]} | slice | bytes 20971520 | tf_op jit(solution)/shard_map/slice | solution.py:163
  402.2 12.7 %all-to-all-done.2 = bf16[4,2,69120]{2,1,0:T(2,128)(2,1)S(1)} async-done(((bf16[4,2,69120]{2,1,0:T(2,128)(2,1)}), bf16[4,2,69120]{2,1,0:T(2,128)(2,1)S(1)}, u32[]{:S(2)}, u32[]{:S(2)}) %all-to-all-start.2) | async-done | bytes 1105952 | tf_op jit(solution)/shard_map/all_to_all | solution.py:179
  414.9 19.6 %reshape.1312 = bf16[2304,1,6,2,20]{4,3,2,1,0:T(2,128)(2,1)} reshape(bf16[4,2,69120]{2,1,0:T(2,128)(2,1)S(1)} %all-to-all-done.2) | data formatting | bytes 2211840
  434.5 18.2 %copy.382 = bf16[1,20,2,6,4,576]{5,4,2,3,1,0:T(4,128)(2,1)S(1)} copy(bf16[1,20,2,6,4,576]{1,2,3,5,4,0:T(2,128)(2,1)} %bitcast.547) | data formatting | bytes 2211840 | tf_op jit(solution)/shard_map/all_to_all | solution.py:179
  455.8 5.1 copy.242
  460.9 5.0 all-to-all-start.3
  465.9 10.9 %fusion.126 = (f32[1,8,36,2048]{3,2,0,1:T(8,128)S(1)}, f32[1,8,36,2048]{3,2,0,1:T(8,128)S(1)}) fusion(s32[2048]{0:T(1024)S(1)} %copy-done.29, s32[8,36]{1,0:T(8,128)S(1)} %add_select_fusion.6, s32[2048]{0:T(1024)S(1)} %copy-done.31, s32[8,36]{1,0:T(8,128)S(1)} %mul.535), kind=kLoop, calls=%fused_computation.142 | loop fusion | flops 11206656 | bytes 4737280 | tf_op jit(solution)/shard_map/cos | solution.py:57
  479.1 3.5 fusion.78
  482.5 19.2 %fusion.35 = f32[8,16,2048,20]{2,3,1,0:T(8,128)} fusion(bf16[20,8,16,2048]{3,2,1,0:T(8,128)(2,1)} %copy-done.3, bf16[1,20,20]{1,2,0:T(8,128)(2,1)S(1)} %copy.404), kind=kOutput, calls=%fused_computation.51 | convolution fusion | flops 209715200 | bytes 31458080 | tf_op jit(solution)/shard_map/boxyz,oi->bixyz/dot_general | solution.py:166
  501.7 3.4 all-to-all-done.3
  505.1 4.3 copy.512
  509.4 21.1 %reshape.1119 = bf16[20,2,8,8,16,36]{5,4,1,2,0,3:T(8,128)(2,1)} reshape(bf16[1,20,2,8,8,576]{5,2,3,1,4,0:T(2,128)(2,1)} %bitcast.549) | data formatting | bytes 5898240 | tf_op jit(solution)/shard_map/reshape.55
  530.5 25.4 %fusion.27 = f32[20,8,16,2048,1,1]{3,0,5,4,2,1:T(8,128)} fusion(bf16[20,2,8,8,16,36]{5,4,1,2,0,3:T(8,128)(2,1)} %reshape.1119, bf16[2,8,36,2048,1,1]{3,2,0,1,4,5:T(8,128)(2,1)} %get-tuple-element.22), kind=kOutput, calls=%fused_computation.45 | convolution fusion | flops 6039797760 | bytes 26279936 | tf_op jit(solution)/shard_map/bcpxsyn,psnz->bcxyz/dot_general | solution.py:70
  555.9 40.8 %fusion.10 = bf16[20,8,16,2048]{3,0,2,1:T(8,128)(2,1)} fusion(f32[20,8,16,2048,1,1]{3,0,5,4,2,1:T(8,128)} %fusion.27, f32[8,16,2048,20]{2,3,1,0:T(8,128)} %fusion.35, bf16[1,1,20,8,16,2048]{5,4,3,2,1,0:T(8,128)(2,1)} %slice.56, bf16[20,2,8,8,16,36]{5,4,1,2,0,3:T(8,128)(2,1)} %reshape.1119, bf16[2,8,36,2048,1,1]{3,2,0,1,4,5:T(8,128)(2,1)S(1)} %copy-done.9), kind=kOutput, calls=%fused_computation.19 | convolution fusion | flops 6107955200 | bytes 68222976 | tf_op jit(solution)/shard_map/bcpxsyn,psnz->bcxyz/dot_general | solution.py:69
  596.7 16.0 %fusion.19 = f32[2,288,20,8,16]{1,2,4,3,0:T(8,128)} fusion(bf16[20,8,16,2048]{3,0,2,1:T(8,128)(2,1)} %fusion.10, f32[2048,1,288]{0,2,1:T(8,128)} %copy-done.11, f32[2048,1,288]{0,2,1:T(8,128)} %copy-done.10), kind=kOutput, calls=%fused_computation.37 | convolution fusion | flops 6045696000 | bytes 21102592 | tf_op jit(solution)/shard_map/bcxyz,zpm->bcpxmy/dot_general | solution.py:70
  612.6 15.3 %fusion.59 = bf16[1,20,2,8,288,16]{4,1,5,3,2,0:T(8,128)(2,1)} fusion(f32[2,288,20,8,16]{1,2,4,3,0:T(8,128)} %fusion.19, bf16[20,8,16,2048]{3,0,2,1:T(8,128)(2,1)S(1)} %copy-done.4, f32[2048,1,288]{0,2,1:T(8,128)} %copy-done.11, f32[2048,1,288]{0,2,1:T(8,128)} %copy-done.10), kind=kOutput, calls=%fused_computation.85 | convolution fusion | flops 6047465472 | bytes 24051712 | tf_op jit(solution)/shard_map/bcxyz,zpm->bcpxmy/dot_general | solution.py:69
  627.9 20.4 %copy.386 = bf16[1,20,2,8,288,16]{1,3,2,5,4,0:T(8,128)(2,1)} copy(bf16[1,20,2,8,288,16]{4,1,5,3,2,0:T(8,128)(2,1)} %fusion.59) | data formatting | bytes 5898240 | tf_op jit(solution)/shard_map/convert_element_type | solution.py:95
  648.3 42.7 %reshape.1313 = bf16[8,2,92160]{2,1,0:T(2,128)(2,1)S(1)} reshape(bf16[4608,1,2,8,20]{4,3,2,1,0:T(8,128)(2,1)} %bitcast.539) | data formatting | bytes 5898240
  691.0 39.1 %all_to_all.120 = bf16[8,2,92160]{2,1,0:T(2,128)(2,1)} all-to-all(bf16[8,2,92160]{2,1,0:T(2,128)(2,1)S(1)} %reshape.1313), channel_id=1, replica_groups=mesh['aa'=8,'ba'=4] {'aa'}, dimensions={0} | all-to-all | bytes 5898240 | tf_op jit(solution)/shard_map/all_to_all | solution.py:98
  730.1 49.8 %reshape.1314 = bf16[4608,1,2,8,20]{4,3,2,1,0:T(8,128)(2,1)} reshape(bf16[8,2,92160]{2,1,0:T(2,128)(2,1)} %all_to_all.120) | data formatting | bytes 5898240
  779.9 18.9 %copy.387 = bf16[1,20,2,8,8,576]{5,4,3,2,1,0:T(8,128)(2,1)S(1)} copy(bf16[1,20,2,8,8,576]{1,3,2,5,4,0:T(8,128)(2,1)} %bitcast.541) | data formatting | bytes 5898240 | tf_op jit(solution)/shard_map/all_to_all | solution.py:98
  801.0 32.6 %all_to_all.121 = bf16[1,20,2,24,576]{4,2,1,0,3:T(2,128)(2,1)S(1)} all-to-all(bf16[1,20,2,24,576]{4,2,1,0,3:T(2,128)(2,1)S(1)} %copy.253), channel_id=1, replica_groups=mesh['aa'=8,'ba'=4] {'ba'}, dimensions={3} | all-to-all | bytes 2211840 | tf_op jit(solution)/shard_map/all_to_all | solution.py:101
  835.0 8.8 reshape.1121
  843.8 10.3 %fusion.46 = f32[2,24,20,6,36,1,1]{4,1,6,3,5,2,0:T(8,128)S(1)} fusion(bf16[20,2,6,4,36,16]{5,4,3,2,1,0:T(8,128)(2,1)} %reshape.1121, f32[1,4,16,1,24]{4,2,1,0,3:T(8,128)S(1)} %copy-done.23, f32[1,4,16,1,24]{4,2,1,0,3:T(8,128)S(1)} %copy-done.21, f32[1,4,16,1,24]{4,2,1,0,3:T(8,128)S(1)} %copy-done.19), kind=kOutput, calls=%fused_computation.62 | convolution fusion | flops 53133312 | bytes 1953792 | tf_op jit(solution)/shard_map/bcpksmu,psuqj->bcqkmj/dot_general | solution.py:69
  854.1 7.7 fusion.117
  861.8 3.2 copy.258
  865.1 3.0 convert_element_type.383
  869.0 13.7 %fusion.42 = (f32[6,864,20]{1,2,0:T(8,128)S(1)}, f32[6,864,20]{1,2,0:T(8,128)S(1)}, f32[6,864,20]{1,2,0:T(8,128)S(1)}, f32[6,864,20]{1,2,0:T(8,128)S(1)}) fusion(f32[6,864,20]{1,0,2:T(8,128)S(1)} %copy.413, bf16[1,1,20,20,6,864]{5,1,4,3,2,0:T(2,128)(2,1)} %get-tuple-element.18, f32[6,864,20]{1,0,2:T(8,128)S(1)} %copy.414, ...), kind=kLoop, calls=%fused_computation.58 | loop fusion | flops 20321280 | bytes 10782720 | tf_op jit(solution)/shard_map/bokr,oikr->bikr/dot_general | solution.py:118
  884.5 4.2 reshape.1290
  888.7 4.3 copy.363
  893.1 2.3 fusion.205
  895.9 2.6 copy.398
  898.4 4.3 reshape.1315
  902.8 3.3 all-to-all-start.6
  906.1 17.1 %fusion.184 = f32[8,16,2048,20]{2,3,1,0:T(8,128)} fusion(bf16[20,8,16,2048]{3,0,2,1:T(8,128)(2,1)} %fusion.10, bf16[1,20,20]{2,0,1:T(2,128)(2,1)S(1)} %copy-done.33), kind=kOutput, calls=%fused_computation.234 | convolution fusion | flops 209715200 | bytes 31458080 | tf_op jit(solution)/shard_map/boxyz,oi->bixyz/dot_general | solution.py:166
  924.7 3.5 reshape.1316
  928.2 2.0 copy.399
  931.6 3.6 all-to-all-start.7
  935.3 27.4 %fusion.7 = f32[1,8,16,2048]{3,0,2,1:T(1,128)} fusion(f32[8,16,2048,20]{2,3,1,0:T(8,128)} %fusion.184, f32[20]{0:T(128)S(1)} %copy-done), kind=kOutput, calls=%fused_computation.15 | convolution fusion | flops 62914560 | bytes 22020176 | tf_op jit(solution)/shard_map/bcxyz,c->bxyz/dot_general | solution.py:204
  963.4 5.8 fusion.95
  (145 shorter events, 30.2 us)
Async XLA Ops:
  0.0 893.0 %copy-start = (f32[20]{0:T(128)S(1)}, f32[20]{0:T(128)}, u32[]{:S(2)}) copy-start(f32[20]{0:T(128)} %param.9) | copy-start | bytes 244
  2.0 27.0 %copy-start.28 = (s32[2048]{0:T(1024)}, s32[2048]{0:T(1024)S(1)}, u32[]{:S(2)}) copy-start(s32[2048]{0:T(1024)S(1)} %get-tuple-element.70) | copy-start | bytes 24580
  2.0 27.0 %copy-start.30 = (s32[2048]{0:T(1024)}, s32[2048]{0:T(1024)S(1)}, u32[]{:S(2)}) copy-start(s32[2048]{0:T(1024)S(1)} %get-tuple-element.71) | copy-start | bytes 24580
  13.7 25.0 %copy-start.3 = (bf16[20,8,16,2048]{3,2,1,0:T(8,128)(2,1)}, bf16[20,8,16,2048]{3,2,1,0:T(8,128)(2,1)S(1)}, u32[]{:S(2)}) copy-start(bf16[20,8,16,2048]{3,2,1,0:T(8,128)(2,1)S(1)} %fusion.37) | copy-start | bytes 31457284
  38.7 16.4 %copy-start.10 = (f32[2048,1,288]{0,2,1:T(8,128)}, f32[2048,1,288]{0,2,1:T(8,128)S(1)}, u32[]{:S(2)}) copy-start(f32[2048,1,288]{0,2,1:T(8,128)S(1)} %get-tuple-element.29) | copy-start | bytes 7077892
  38.7 16.4 %copy-start.11 = (f32[2048,1,288]{0,2,1:T(8,128)}, f32[2048,1,288]{0,2,1:T(8,128)S(1)}, u32[]{:S(2)}) copy-start(f32[2048,1,288]{0,2,1:T(8,128)S(1)} %get-tuple-element.30) | copy-start | bytes 7077892
  142.0 41.2 %all-to-all-start = ((bf16[8,2,92160]{2,1,0:T(2,128)(2,1)}), bf16[8,2,92160]{2,1,0:T(2,128)(2,1)S(1)}, u32[]{:S(2)}, u32[]{:S(2)}) async-start(bf16[8,2,92160]{2,1,0:T(2,128)(2,1)} %reshape.1309), calls=%async_computation | async-start | bytes 5898240 | tf_op jit(solution)/shard_map/all_to_all | solution.py:98
  147.6 105.4 %copy-start.24 = (f32[1,64,2,24]{1,3,0,2:T(8,128)}, f32[1,64,2,24]{1,3,0,2:T(8,128)S(1)}, u32[]{:S(2)}) copy-start(f32[1,64,2,24]{1,3,0,2:T(8,128)S(1)} %get-tuple-element.33) | copy-start | bytes 36868
  147.6 105.4 %copy-start.26 = (f32[1,64,2,24]{1,3,0,2:T(8,128)}, f32[1,64,2,24]{1,3,0,2:T(8,128)S(1)}, u32[]{:S(2)}) copy-start(f32[1,64,2,24]{1,3,0,2:T(8,128)S(1)} %get-tuple-element.34) | copy-start | bytes 36868
  255.7 40.7 %all-to-all-start.1 = ((bf16[1,20,2,24,576]{4,2,1,0,3:T(2,128)(2,1)}), bf16[1,20,2,24,576]{4,2,1,0,3:T(2,128)(2,1)S(1)}, u32[]{:S(2)}, u32[]{:S(2)}) async-start(bf16[1,20,2,24,576]{4,2,1,0,3:T(2,128)(2,1)} %copy.224), calls=%async_computation.1 | async-start | bytes 2457600 | tf_op jit(solution)/shard_map/all_to_all | solution.py:101
  296.1 158.6 %copy-start.12 = (f32[1,24,2,64]{3,1,0,2:T(8,128)}, f32[1,24,2,64]{3,1,0,2:T(8,128)S(1)}, u32[]{:S(2)}) copy-start(f32[1,24,2,64]{3,1,0,2:T(8,128)S(1)} %get-tuple-element.31) | copy-start | bytes 36868
  296.2 158.6 %copy-start.15 = (f32[1,24,2,64]{3,1,0,2:T(8,128)}, f32[1,24,2,64]{3,1,0,2:T(8,128)S(1)}, u32[]{:S(2)}) copy-start(f32[1,24,2,64]{3,1,0,2:T(8,128)S(1)} %get-tuple-element.32) | copy-start | bytes 36868
  296.4 20.5 %copy-start.18 = (f32[1,4,16,1,24]{4,2,1,0,3:T(8,128)}, f32[1,4,16,1,24]{4,2,1,0,3:T(8,128)S(1)}, u32[]{:S(2)}) copy-start(f32[1,4,16,1,24]{4,2,1,0,3:T(8,128)S(1)} %get-tuple-element.37) | copy-start | bytes 18436
  296.4 20.5 %copy-start.20 = (f32[1,4,16,1,24]{4,2,1,0,3:T(8,128)}, f32[1,4,16,1,24]{4,2,1,0,3:T(8,128)S(1)}, u32[]{:S(2)}) copy-start(f32[1,4,16,1,24]{4,2,1,0,3:T(8,128)S(1)} %get-tuple-element.38) | copy-start | bytes 18436
  296.4 20.5 %copy-start.22 = (f32[1,4,16,1,24]{4,2,1,0,3:T(8,128)}, f32[1,4,16,1,24]{4,2,1,0,3:T(8,128)S(1)}, u32[]{:S(2)}) copy-start(f32[1,4,16,1,24]{4,2,1,0,3:T(8,128)S(1)} %get-tuple-element.39) | copy-start | bytes 18436
  306.6 10.3 %copy-start.2 = (bf16[20,2,6,4,36,16]{5,4,3,2,1,0:T(8,128)(2,1)S(1)}, bf16[20,2,6,4,36,16]{5,4,3,2,1,0:T(8,128)(2,1)}, u32[]{:S(2)}) copy-start(bf16[20,2,6,4,36,16]{5,4,3,2,1,0:T(8,128)(2,1)} %reshape.1115) | copy-start | bytes 3317764
  349.5 0.9 copy-start.8
  385.8 29.2 %all-to-all-start.2 = ((bf16[4,2,69120]{2,1,0:T(2,128)(2,1)}), bf16[4,2,69120]{2,1,0:T(2,128)(2,1)S(1)}, u32[]{:S(2)}, u32[]{:S(2)}) async-start(bf16[4,2,69120]{2,1,0:T(2,128)(2,1)} %reshape.1311), calls=%async_computation.2 | async-start | bytes 2211840 | tf_op jit(solution)/shard_map/all_to_all | solution.py:179
  391.3 10.1 %copy-start.32 = (bf16[2,20,20]{2,0,1:T(2,128)(2,1)S(1)}, bf16[2,20,20]{2,0,1:T(2,128)(2,1)}, u32[]{:S(2)}) copy-start(bf16[2,20,20]{2,0,1:T(2,128)(2,1)} %param.8) | copy-start | bytes 4804
  460.9 5.0 copy-start.29
  460.9 5.0 copy-start.31
  460.9 44.2 %all-to-all-start.3 = ((bf16[1,20,2,64,576]{4,2,1,0,3:T(2,128)(2,1)}), bf16[1,20,2,64,576]{4,2,1,0,3:T(2,128)(2,1)S(1)}, u32[]{:S(2)}, u32[]{:S(2)}) async-start(bf16[1,20,2,64,576]{4,2,1,0,3:T(2,128)(2,1)} %copy.242), calls=%async_computation.3 | async-start | bytes 6553600 | tf_op jit(solution)/shard_map/all_to_all | solution.py:182
  476.8 1.5 copy-start.5
  476.8 2.3 copy-start.7
  530.5 25.4 %copy-start.9 = (bf16[2,8,36,2048,1,1]{3,2,0,1,4,5:T(8,128)(2,1)S(1)}, bf16[2,8,36,2048,1,1]{3,2,0,1,4,5:T(8,128)(2,1)}, u32[]{:S(2)}) copy-start(bf16[2,8,36,2048,1,1]{3,2,0,1,4,5:T(8,128)(2,1)} %get-tuple-element.21) | copy-start | bytes 7077892
  596.7 16.0 %copy-start.4 = (bf16[20,8,16,2048]{3,0,2,1:T(8,128)(2,1)S(1)}, bf16[20,8,16,2048]{3,0,2,1:T(8,128)(2,1)}, u32[]{:S(2)}) copy-start(bf16[20,8,16,2048]{3,0,2,1:T(8,128)(2,1)} %fusion.10) | copy-start | bytes 31457284
  779.9 18.9 %copy-start.25 = (f32[1,64,2,24]{1,3,0,2:T(8,128)S(1)}, f32[1,64,2,24]{1,3,0,2:T(8,128)}, u32[]{:S(2)}) copy-start(f32[1,64,2,24]{1,3,0,2:T(8,128)} %copy-done.24) | copy-start | bytes 36868
  779.9 18.9 %copy-start.27 = (f32[1,64,2,24]{1,3,0,2:T(8,128)S(1)}, f32[1,64,2,24]{1,3,0,2:T(8,128)}, u32[]{:S(2)}) copy-start(f32[1,64,2,24]{1,3,0,2:T(8,128)} %copy-done.26) | copy-start | bytes 36868
  835.0 8.8 copy-start.19
  835.0 8.8 copy-start.21
  835.0 8.8 copy-start.23
  843.8 10.3 %copy-start.1 = (bf16[20,2,6,4,36,16]{5,4,3,2,1,0:T(8,128)(2,1)S(1)}, bf16[20,2,6,4,36,16]{5,4,3,2,1,0:T(8,128)(2,1)}, u32[]{:S(2)}) copy-start(bf16[20,2,6,4,36,16]{5,4,3,2,1,0:T(8,128)(2,1)} %reshape.1121) | copy-start | bytes 3317764
  893.0 2.3 copy-start.13
  893.1 2.3 copy-start.16
  895.4 10.7 %copy-start.33 = (bf16[1,20,20]{2,0,1:T(2,128)(2,1)S(1)}, bf16[1,20,20]{2,0,1:T(2,128)(2,1)}, u32[]{:S(2)}) copy-start(bf16[1,20,20]{2,0,1:T(2,128)(2,1)} %get-tuple-element.35) | copy-start | bytes 2404
  902.8 20.5 %all-to-all-start.6 = ((f32[4,1,6912]{2,1,0:T(1,128)}), f32[4,1,6912]{2,1,0:T(1,128)S(1)}, u32[]{:S(2)}, u32[]{:S(2)}) async-start(f32[4,1,6912]{2,1,0:T(1,128)} %reshape.1315), calls=%async_computation.6 | async-start | bytes 221184 | tf_op jit(solution)/shard_map/all_to_all | solution.py:196
  923.2 7.1 copy-start.14
  923.2 7.1 copy-start.17
  931.6 31.0 %all-to-all-start.7 = ((bf16[1,1,2,64,576]{4,2,1,0,3:T(2,128)(2,1)}), bf16[1,1,2,64,576]{4,2,1,0,3:T(2,128)(2,1)S(1)}, u32[]{:S(2)}, u32[]{:S(2)}) async-start(bf16[1,1,2,64,576]{4,2,1,0,3:T(2,128)(2,1)} %copy.271), calls=%async_computation.7 | async-start | bytes 327680 | tf_op jit(solution)/shard_map/all_to_all | solution.py:199
  935.3 28.1 %copy-start.6 = (f32[1,8,36,2048]{3,2,0,1:T(8,128)S(1)}, f32[1,8,36,2048]{3,2,0,1:T(8,128)}, u32[]{:S(2)}) copy-start(f32[1,8,36,2048]{3,2,0,1:T(8,128)} %copy-done.5) | copy-start | bytes 7077892
where the time goes:
time: 980 us; the launch traced here: 970 us
  local copies, waits for them, and re-layouts  482 us (49%)
  matrix products  253 us (26%)
  other arithmetic  81.7 us (8%)
  blocking collectives  71.8 us (7%)
  waiting for transfers between devices  51.6 us (5%)
  starting transfers between devices  28.2 us (3%)
    unnamed x81, local copies, waits for them, and re-layouts  235 us
    dot_general x9, matrix products, split_product(): jnp.einsum(pattern, values, halves_pair[0], preferred_element_type=jnp.fl...  103 us
    dot_general x9, matrix products, split_product(): jnp.einsum(pattern, values, halves_pair[1], preferred_element_type=jnp.fl...  77.4 us
    another operation x6, local copies, waits for them, and re-layouts  47.9 us
    convert_element_type x2, local copies, waits for them, and re-layouts, forward_modes(): plane_spectrum = plane_spectrum.reshape(extent[0], extent[1], 2, extent[3...  40.8 us
    all_to_all x1, blocking collectives, forward_modes(): lax.all_to_all(plane_spectrum, 'aa', split_axis=4, concat_axis=3, tiled=T...  39.1 us
    all_to_all x2, local copies, waits for them, and re-layouts, forward_modes(): lax.all_to_all(plane_spectrum, 'aa', split_axis=4, concat_axis=3, tiled=T...  37.7 us
    dot_general x2, matrix products, per_device(): jnp.einsum('boxyz,oi->bixyz', grad_pre, skip_weights[layer_index], prefer...  36.3 us
  transfers between devices with their start and end apart: 6, of which 3 were waited for; matrix products, arithmetic and copies ran while one was open for 13% of the time, Pallas kernels for 0%

commit v1 on v0

v1 whole, which is shorter than its diff:
```python
import math

import jax
import jax.numpy as jnp
import numpy as np
from jax import lax
from jax.sharding import PartitionSpec as P

NX = 64
NY = 64
NZ = 64
NT = 32
KX = 24
KY = 24
KZ = 24
KT = 12


def gelu_slope(values):
    normal_cdf = 0.5 * (1.0 + lax.erf(values / math.sqrt(2.0)))
    density = jnp.exp(-0.5 * values * values) / math.sqrt(2.0 * math.pi)
    return normal_cdf + values * density


def signed_freq(total_count):
    index_list = np.arange(total_count)
    return np.where(index_list < total_count // 2, index_list, index_list - total_count)


def line_tables(total_count, length):
    turns = signed_freq(total_count)[:, None] * np.arange(length)[None, :] % length
    angles = 2.0 * math.pi / length * turns
    cosine = np.cos(angles)
    sine_part = np.sin(angles)
    forward = np.stack(
        [np.stack([cosine.T, -sine_part.T], 1), np.stack([sine_part.T, cosine.T], 1)], 0
    )
    inverse = (
        np.stack([np.stack([cosine, sine_part], 1), np.stack([-sine_part, cosine], 1)], 0)
        / length
    )
    return (forward, inverse)


def plane_tables():
    joint_index = np.arange(KZ * KT)
    depth_freq = signed_freq(KZ)[joint_index // KT]
    time_freq = joint_index % KT
    cell_index = np.arange(NZ * NT)
    turns = (
        depth_freq[:, None] * (cell_index // NT)[None, :] * NT
        + time_freq[:, None] * (cell_index % NT)[None, :] * NZ
    ) % (NZ * NT)
    angles = 2.0 * math.pi / (NZ * NT) * turns
    forward = np.stack([np.cos(angles).T, -np.sin(angles).T], 1)
    inverse = np.stack([np.cos(angles), -np.sin(angles)], 0) / (NZ * NT)
    return (forward, inverse)


def rounded_product(pattern, values, table):
    return jnp.einsum(
        pattern, values, jnp.asarray(table, jnp.bfloat16), preferred_element_type=jnp.float32
    )


def exact_product(pattern, values, table):
    return jnp.einsum(
        pattern, values, jnp.asarray(table, jnp.float32), precision=lax.Precision.HIGHEST
    )


def to_bf16(values):
    return values.astype(jnp.bfloat16)


def keep_float(values):
    return values


def exchange(values, axis):
    return lax.all_to_all(values, axis, split_axis=0, concat_axis=0, tiled=True)


def forward_modes(grad_pre, weights, tables):
    plane, first, second = tables
    rows = lax.axis_size("aa")
    columns = lax.axis_size("ba")
    plane = plane.reshape(NZ * NT, 2, rows, -1)
    spectrum = to_bf16(rounded_product("bcxyz,zpnm->nbcpxmy", grad_pre, plane))
    blocks = exchange(spectrum, "aa")
    first = first.reshape(2, rows, NX // rows, 2, columns, KX // columns)
    spectrum = to_bf16(rounded_product("nbcpxmy,pnxqgk->gbcqkmy", blocks, first))
    blocks = exchange(spectrum, "ba")
    second = second.reshape(2, columns, NY // columns, 2, KY)
    result = to_bf16(rounded_product("gbcpkmy,pgyqj->bcqkmj", blocks, second))
    shape = result.shape
    spectrum = result.reshape(shape[:4] + (shape[4] * KY,))
    real_part = spectrum[:, :, 0]
    imag_part = spectrum[:, :, 1]

    def mixing(values, matrix):
        return jnp.einsum("bokr,oikr->bikr", values, matrix, preferred_element_type=jnp.float32)

    result_real = mixing(real_part, weights[0]) + mixing(imag_part, weights[1])
    result_imag = mixing(imag_part, weights[0]) - mixing(real_part, weights[1])
    return jnp.stack([result_real, result_imag], 2)


def back_path(mode_values, tables, multiply, finish):
    first, second, plane = tables
    rows = lax.axis_size("aa")
    columns = lax.axis_size("ba")
    extent = mode_values.shape
    gridded = mode_values.reshape(extent[:4] + (extent[4] // KY, KY))
    second = second.reshape(2, KY, 2, columns, NY // columns)
    blocks = exchange(finish(multiply("bcpkmj,pjqgu->gbcqkmu", gridded, second)), "ba")
    first = first.reshape(2, columns, KX // columns, 2, rows, NX // rows)
    back = to_bf16(multiply("gbcpkmu,pgkqnx->nbcqxmu", blocks, first))
    blocks = exchange(back, "aa")
    plane = plane.reshape(2, rows, -1, NZ * NT)
    return rounded_product("nbcpxmu,pnmz->bcxuz", blocks, plane)


def per_device(cotangent, pre_activations, spectral_weights, skip_weights, lift_weights):
    plane_forward, plane_inverse = plane_tables()
    first_forward, first_inverse = line_tables(KX, NX)
    second_forward, second_inverse = line_tables(KY, NY)
    forward_tables = (plane_forward, first_forward, second_forward)
    back_tables = (first_inverse, second_inverse, plane_inverse)
    incoming = cotangent.astype(jnp.float32)
    layers = pre_activations.shape[0]
    perm_grad = None
    for layer_index in range(layers - 1, -1, -1):
        slope = gelu_slope(pre_activations[layer_index].astype(jnp.float32))
        grad_pre = (incoming * slope).astype(jnp.bfloat16)
        mode_values = forward_modes(grad_pre, spectral_weights[layer_index], forward_tables)
        if layer_index > 0:
            skip_term = jnp.einsum(
                "boxyz,oi->bixyz",
                grad_pre,
                skip_weights[layer_index],
                preferred_element_type=jnp.float32,
            )
            spectral = back_path(
                mode_values.astype(jnp.bfloat16), back_tables, rounded_product, to_bf16
            )
            incoming = skip_term + spectral
        else:
            folded = jnp.sum(mode_values * lift_weights[None, :, None, None, None], 1)[:, None]
            spectral = back_path(folded, back_tables, exact_product, keep_float)
            combined = jnp.sum(skip_weights[0].astype(jnp.float32) * lift_weights[None, :], 1)
            projected = jnp.sum(
                grad_pre.astype(jnp.float32) * combined[None, :, None, None, None], 1
            )
            perm_grad = projected + spectral[:, 0]
    return perm_grad


def solution(mesh):
    return jax.shard_map(
        per_device,
        mesh=mesh,
        in_specs=(
            P(None, None, "aa", "ba", None),
            P(None, None, None, "aa", "ba", None),
            P(None, None, None, None, "ba", "aa"),
            P(),
            P(),
        ),
        out_specs=P(None, "aa", "ba", None),
        check_vma=False,
    )
```

time: 980 us -> 760 us (0.78)
  local copies, waits for them, and re-layouts: 482 us -> 366 us
  blocking collectives: 71.8 us -> 158 us
  matrix products: 253 us -> 169 us
  waiting for transfers between devices: 51.6 us -> 6.03 us
  other arithmetic: 81.7 us -> 41.7 us
  starting transfers between devices: 28.2 us -> 8.86 us
    all_to_all x2 -> x6, blocking collectives: 71.8 us -> 158 us  [exchange(): return lax.all_to_all(values, axis, split_axis=0, concat_axis=0, tiled=True)]
    dot_general x23 -> x12, matrix products: 216 us -> 150 us  [the longest x10 147 us: rounded_product(): jnp.einsum(pattern, values, jnp.asarray(table, jnp.bfloat16), preferred_e...]
    all_to_all x12 -> x1, local copies, waits for them, and re-layouts: 66.4 us -> 0.59 us  [exchange(): return lax.all_to_all(values, axis, split_axis=0, concat_axis=0, tiled=True)]
    convert_element_type x9 -> x0, local copies, waits for them, and re-layouts: 57 us -> none  [the longest x2 40.8 us: forward_modes(): plane_spectrum = plane_spectrum.reshape(extent[0], extent[1], 2, extent[3...]
    all_to_all x6 -> x2, waiting for transfers between devices: 51.6 us -> 6.03 us  [exchange(): return lax.all_to_all(values, axis, split_axis=0, concat_axis=0, tiled=True)]
    another operation x6 -> x2, local copies, waits for them, and re-layouts: 47.9 us -> 12.2 us
    convert_element_type x2 -> x9, local copies, waits for them, and re-layouts: 20.8 us -> 55.2 us  [to_bf16(): return values.astype(jnp.bfloat16)]
    cos x2 -> x0, other arithmetic: 20.5 us -> none  [plane_tables(): forward = jnp.stack([jnp.cos(angles).T, -jnp.sin(angles).T], 1)]
  transfers between devices with their start and end apart: 6 -> 2, of which waited for: 3 -> 1; matrix products, arithmetic and copies ran while one was open for 13% -> 9% of each run, Pallas kernels for 0% -> 0%
where the time goes in v1:
time: 760 us; the launch traced here: 751 us
  local copies, waits for them, and re-layouts  366 us (48%)
  matrix products  169 us (22%)
  blocking collectives  158 us (21%)
  other arithmetic  41.7 us (5%)
  starting transfers between devices  8.86 us (1%)
    unnamed x49, local copies, waits for them, and re-layouts  241 us
    all_to_all x6, blocking collectives, exchange(): return lax.all_to_all(values, axis, split_axis=0, concat_axis=0, tiled=True)  158 us
    dot_general x10, matrix products, rounded_product(): jnp.einsum(pattern, values, jnp.asarray(table, jnp.bfloat16), preferred_e...  147 us
    convert_element_type x9, local copies, waits for them, and re-layouts, to_bf16(): return values.astype(jnp.bfloat16)  55.2 us
    slice x1, local copies, waits for them, and re-layouts, forward_modes(): result_real = mixing(real_part, weights[0]) + mixing(imag_part, weights[1])  34.9 us
    dot_general x2, other arithmetic, mixing(): jnp.einsum('bokr,oikr->bikr', values, matrix, preferred_element_type=jnp....  27.4 us
    dot_general x1, matrix products, per_device(): jnp.einsum('boxyz,oi->bixyz', grad_pre, skip_weights[layer_index], prefer...  19.2 us
  transfers between devices with their start and end apart: 2, of which 1 were waited for; matrix products, arithmetic and copies ran while one was open for 9% of the time, Pallas kernels for 0%

profile of v1, /device:TPU:0, one launch (start us, length us, event | category | flops | bytes accessed | tf_op | source)
XLA Modules:
  0.0 751.2 jit_solution(14171039238767741179)
XLA Ops:
  0.0 11.8 %fusion.15 = bf16[1,20,8,16,2048]{4,3,2,1,0:T(8,128)(2,1)S(1)} fusion(bf16[1,20,8,16,2048]{4,3,2,1,0:T(8,128)(2,1)} %param.17, bf16[2,1,20,8,16,2048]{5,4,3,2,1,0:T(8,128)(2,1)} %param.18), kind=kLoop, calls=%fused_computation.26 | loop fusion | flops 62914560 | bytes 31457280 | tf_op jit(solution)/shard_map/convert_element_type | solution.py:135
  11.8 3.9 copy-done
  15.7 24.3 %convert_bitcast_fusion.1 = bf16[8,1,20,2,8,36,16]{5,6,0,3,4,2,1:T(8,128)(2,1)} fusion(bf16[2048,2,8,36,1,1]{0,3,2,1,5,4:T(8,128)(2,1)S(1)} %copy-done.9, bf16[1,20,8,16,2048]{4,3,2,1,0:T(8,128)(2,1)S(1)} %fusion.15), kind=kOutput, calls=%fused_computation.54 | convolution fusion | flops 6041272320 | bytes 15794176 | tf_op jit(solution)/shard_map/bcxyz,zpnm->nbcpxmy/dot_general | solution.py:61
  39.9 10.9 %copy.358 = bf16[8,1,20,2,8,36,16]{5,6,3,4,2,1,0:T(8,128)(2,1)} copy(bf16[8,1,20,2,8,36,16]{5,6,0,3,4,2,1:T(8,128)(2,1)} %convert_bitcast_fusion.1) | data formatting | bytes 5898240 | tf_op jit(solution)/shard_map/convert_element_type | solution.py:73
  50.9 25.2 %reshape.320 = bf16[8,2,92160]{2,1,0:T(2,128)(2,1)S(1)} reshape(bf16[8,1,20,8,2,16,36]{6,5,4,3,2,1,0:T(8,128)(2,1)} %bitcast.398) | data formatting | bytes 5898240
  76.1 41.4 %all_to_all.40 = bf16[8,2,92160]{2,1,0:T(2,128)(2,1)} all-to-all(bf16[8,2,92160]{2,1,0:T(2,128)(2,1)S(1)} %reshape.320), channel_id=1, replica_groups=mesh['aa'=8,'ba'=4] {'aa'}, dimensions={0} | all-to-all | bytes 5898240 | tf_op jit(solution)/shard_map/all_to_all | solution.py:81
  117.5 30.4 %reshape.321 = bf16[8,1,20,8,2,16,36]{6,5,4,3,2,1,0:T(8,128)(2,1)} reshape(bf16[8,2,92160]{2,1,0:T(2,128)(2,1)} %all_to_all.40) | data formatting | bytes 5898240
  147.9 8.8 %fusion.45 = bf16[4,1,20,2,6,36,16]{5,4,0,3,6,2,1:T(8,128)(2,1)S(1)} fusion(bf16[2,8,8,2,4,6,1,1]{2,5,0,1,4,3,7,6:T(8,128)(2,1)S(1)} %copy-done.11, bf16[8,1,20,2,8,36,16]{5,6,3,4,2,1,0:T(8,128)(2,1)} %bitcast.405), kind=kOutput, calls=%fused_computation.64 | convolution fusion | flops 142110720 | bytes 4067328 | tf_op jit(solution)/shard_map/nbcpxmy,pnxqgk->gbcqkmy/dot_general | solution.py:61
  156.7 6.4 copy.361
  163.1 10.2 %reshape.322 = bf16[4,2,69120]{2,1,0:T(2,128)(2,1)} reshape(bf16[4,1,20,2,6,16,36]{6,5,4,3,2,1,0:T(8,128)(2,1)} %bitcast.401) | data formatting | bytes 2211840
  173.3 5.0 all-to-all-start.1
  178.4 34.9 %fusion.85 = (bf16[1,1,20,20,6,864]{5,1,4,3,2,0:T(2,128)(2,1)}, bf16[1,1,20,20,6,864]{5,1,4,3,2,0:T(2,128)(2,1)}, bf16[1,1,20,20,6,864]{5,1,4,3,2,0:T(2,128)(2,1)}, bf16[1,1,20,20,6,864]{5,1,4,3,2,0:T(2,128)(2,1)}) fusion(bf16[2,2,20,20,6,864]{5,1,4,3,2,0:T(2,128)(2,1)} %param.19), kind=kLoop, calls=%fused_computation.114 | loop fusion | bytes 33177600 | tf_op jit(solution)/shard_map/slice | solution.py:104
  213.3 11.9 %reshape.323 = bf16[4,1,20,2,6,16,36]{6,5,4,3,2,1,0:T(8,128)(2,1)} reshape(bf16[4,2,69120]{2,1,0:T(2,128)(2,1)S(1)} %all-to-all-done.1) | data formatting | bytes 2211840
  225.2 3.9 fusion.68
  229.2 3.3 copy.122
  232.4 3.0 reshape.258
  235.4 0.6 fusion.87
  236.3 13.7 %fusion.33 = (f32[6,864,20]{1,2,0:T(8,128)S(1)}, f32[6,864,20]{1,2,0:T(8,128)S(1)}, f32[6,864,20]{1,2,0:T(8,128)S(1)}, f32[6,864,20]{1,2,0:T(8,128)S(1)}) fusion(f32[6,864,20]{1,0,2:T(8,128)S(1)} %copy.260, bf16[1,1,20,20,6,864]{5,1,4,3,2,0:T(2,128)(2,1)} %get-tuple-element.20, f32[6,864,20]{1,0,2:T(8,128)S(1)} %copy.261, ...), kind=kLoop, calls=%fused_computation.55 | loop fusion | flops 20321280 | bytes 10782720 | tf_op jit(solution)/shard_map/bokr,oikr->bikr/dot_general | solution.py:102
  250.1 0.9 stack.18
  251.0 1.0 copy.127
  252.1 0.9 stack.19
  253.0 1.0 copy.128
  254.0 1.2 fusion.49
  255.3 3.0 copy.360
  258.3 9.5 %reshape.324 = bf16[4,2,69120]{2,1,0:T(2,128)(2,1)S(1)} reshape(bf16[4,1,20,6,2,16,36]{6,5,4,3,2,1,0:T(8,128)(2,1)} %bitcast.402) | data formatting | bytes 2211840
  267.8 31.6 %all_to_all.41 = bf16[4,2,69120]{2,1,0:T(2,128)(2,1)S(1)} all-to-all(bf16[4,2,69120]{2,1,0:T(2,128)(2,1)S(1)} %reshape.324), channel_id=1, replica_groups=mesh['aa'=8,'ba'=4] {'ba'}, dimensions={0} | all-to-all | bytes 2211840 | tf_op jit(solution)/shard_map/all_to_all | solution.py:81
  299.5 11.9 %reshape.325 = bf16[4,1,20,6,2,16,36]{6,5,4,3,2,1,0:T(8,128)(2,1)} reshape(bf16[4,2,69120]{2,1,0:T(2,128)(2,1)S(1)} %all_to_all.41) | data formatting | bytes 2211840
  311.4 8.3 %fusion.22 = bf16[8,1,20,2,8,36,16]{5,4,0,3,6,2,1:T(8,128)(2,1)} fusion(bf16[2,4,6,2,8,8,1,1]{2,5,0,1,4,3,7,6:T(8,128)(2,1)S(1)} %copy-done.13, bf16[4,1,20,2,6,36,16]{5,6,3,4,2,1,0:T(8,128)(2,1)} %bitcast.406), kind=kOutput, calls=%fused_computation.40 | convolution fusion | flops 143032320 | bytes 4067328 | tf_op jit(solution)/shard_map/gbcpkmu,pgkqnx->nbcqxmu/dot_general | solution.py:61
  319.7 10.8 %copy.357 = bf16[8,1,20,2,8,36,16]{5,4,3,6,2,1,0:T(8,128)(2,1)} copy(bf16[8,1,20,2,8,36,16]{5,4,0,3,6,2,1:T(8,128)(2,1)} %fusion.22) | data formatting | bytes 5898240 | tf_op jit(solution)/shard_map/convert_element_type | solution.py:73
  330.5 26.0 %reshape.326 = bf16[8,2,92160]{2,1,0:T(2,128)(2,1)} reshape(bf16[8,1,20,16,2,8,36]{6,5,4,3,2,1,0:T(8,128)(2,1)} %bitcast.399) | data formatting | bytes 5898240
  356.5 3.8 all-to-all-start.3
  360.3 10.2 %slice.56 = bf16[1,1,20,8,16,2048]{5,4,3,2,1,0:T(8,128)(2,1)} slice(bf16[2,1,20,8,16,2048]{5,4,3,2,1,0:T(8,128)(2,1)} %param.18), slice={[0:1], [0:1], [0:20], [0:8], [0:16], [0:2048]} | slice | bytes 20971520 | tf_op jit(solution)/shard_map/slice | solution.py:134
  370.8 19.2 %fusion.20 = f32[8,16,2048,20]{2,3,1,0:T(8,128)} fusion(bf16[20,8,16,2048]{3,2,1,0:T(8,128)(2,1)} %bitcast.397, bf16[1,20,20]{1,2,0:T(8,128)(2,1)S(1)} %copy.253), kind=kOutput, calls=%fused_computation.38 | convolution fusion | flops 209715200 | bytes 31458080 | tf_op jit(solution)/shard_map/boxyz,oi->bixyz/dot_general | solution.py:138
  390.0 6.0 all-to-all-done.3
  396.0 30.9 %reshape.327 = bf16[8,1,20,16,2,8,36]{6,5,4,3,2,1,0:T(8,128)(2,1)} reshape(bf16[8,2,92160]{2,1,0:T(2,128)(2,1)S(1)} %all-to-all-done.3) | data formatting | bytes 5898240
  426.9 12.0 %bitcast_bitcast_fusion = bf16[8,20,2,8,36,16]{4,3,2,5,1,0:T(8,128)(2,1)} fusion(bf16[8,1,20,16,2,8,36]{6,5,4,3,2,1,0:T(8,128)(2,1)} %reshape.327), kind=kLoop, calls=%fused_computation.118 | loop fusion | bytes 5898240 | tf_op jit(solution)/shard_map/reshape.28
  438.9 52.2 %multiply_reduce_fusion = (f32[8,16,2048]{2,1,0:T(8,128)}, bf16[20,8,16,2048]{3,0,2,1:T(8,128)(2,1)}) fusion(f32[20]{0:T(128)S(1)} %fusion.82, bf16[1,1,20,8,16,2048]{5,4,3,2,1,0:T(8,128)(2,1)} %slice.56, bf16[2,8,36,2048,1,1]{3,2,0,1,5,4:T(8,128)(2,1)} %constant.54, bf16[8,20,2,8,36,16]{4,3,2,5,1,0:T(8,128)(2,1)} %bitcast_bitcast_fusion, ...), kind=kOutput, calls=%fused_computation.16 | convolution fusion | flops 6118178816 | bytes 48300112 | tf_op jit(solution)/shard_map/nbcpxmu,pnmz->bcxuz/dot_general | solution.py:61
  491.1 32.6 %convert_bitcast_fusion = bf16[8,1,20,2,8,36,16]{5,6,0,3,4,2,1:T(8,128)(2,1)} fusion(bf16[2048,2,8,36,1,1]{0,3,2,1,5,4:T(8,128)(2,1)S(1)} %copy-done.10, bf16[20,8,16,2048,1,1]{3,0,2,1,5,4:T(8,128)(2,1)} %bitcast.411), kind=kOutput, calls=%fused_computation.53 | convolution fusion | flops 6041272320 | bytes 15794176 | tf_op jit(solution)/shard_map/bcxyz,zpnm->nbcpxmy/dot_general | solution.py:61
  523.8 10.9 %copy.356 = bf16[8,1,20,2,8,36,16]{5,6,3,4,2,1,0:T(8,128)(2,1)} copy(bf16[8,1,20,2,8,36,16]{5,6,0,3,4,2,1:T(8,128)(2,1)} %convert_bitcast_fusion) | data formatting | bytes 5898240 | tf_op jit(solution)/shard_map/convert_element_type | solution.py:73
  534.7 25.2 %reshape.328 = bf16[8,2,92160]{2,1,0:T(2,128)(2,1)S(1)} reshape(bf16[8,1,20,8,2,16,36]{6,5,4,3,2,1,0:T(8,128)(2,1)} %bitcast.400) | data formatting | bytes 5898240
  559.9 39.2 %all_to_all.42 = bf16[8,2,92160]{2,1,0:T(2,128)(2,1)} all-to-all(bf16[8,2,92160]{2,1,0:T(2,128)(2,1)S(1)} %reshape.328), channel_id=1, replica_groups=mesh['aa'=8,'ba'=4] {'aa'}, dimensions={0} | all-to-all | bytes 5898240 | tf_op jit(solution)/shard_map/all_to_all | solution.py:81
  599.2 30.4 %reshape.329 = bf16[8,1,20,8,2,16,36]{6,5,4,3,2,1,0:T(8,128)(2,1)} reshape(bf16[8,2,92160]{2,1,0:T(2,128)(2,1)} %all_to_all.42) | data formatting | bytes 5898240
  629.6 8.8 %fusion.46 = bf16[4,1,20,2,6,36,16]{5,4,0,3,6,2,1:T(8,128)(2,1)S(1)} fusion(bf16[2,8,8,2,4,6,1,1]{2,5,0,1,4,3,7,6:T(8,128)(2,1)S(1)} %copy-done.12, bf16[8,1,20,2,8,36,16]{5,6,3,4,2,1,0:T(8,128)(2,1)} %bitcast.404), kind=kOutput, calls=%fused_computation.65 | convolution fusion | flops 142110720 | bytes 4067328 | tf_op jit(solution)/shard_map/nbcpxmy,pnxqgk->gbcqkmy/dot_general | solution.py:61
  638.4 6.4 copy.359
  644.8 9.5 %reshape.330 = bf16[4,2,69120]{2,1,0:T(2,128)(2,1)S(1)} reshape(bf16[4,1,20,2,6,16,36]{6,5,4,3,2,1,0:T(8,128)(2,1)} %bitcast.403) | data formatting | bytes 2211840
  654.3 29.8 %all_to_all.43 = bf16[4,2,69120]{2,1,0:T(2,128)(2,1)S(1)} all-to-all(bf16[4,2,69120]{2,1,0:T(2,128)(2,1)S(1)} %reshape.330), channel_id=1, replica_groups=mesh['aa'=8,'ba'=4] {'ba'}, dimensions={0} | all-to-all | bytes 2211840 | tf_op jit(solution)/shard_map/all_to_all | solution.py:81
  684.1 11.9 %reshape.331 = bf16[4,1,20,2,6,16,36]{6,5,4,3,2,1,0:T(8,128)(2,1)} reshape(bf16[4,2,69120]{2,1,0:T(2,128)(2,1)S(1)} %all_to_all.43) | data formatting | bytes 2211840
  696.0 3.9 fusion.71
  699.9 3.3 copy.141
  703.2 3.0 reshape.265
  706.2 0.6 fusion.86
  707.1 13.7 %fusion.37 = (f32[6,864,20]{1,2,0:T(8,128)S(1)}, f32[6,864,20]{1,2,0:T(8,128)S(1)}, f32[6,864,20]{1,2,0:T(8,128)S(1)}, f32[6,864,20]{1,2,0:T(8,128)S(1)}) fusion(f32[6,864,20]{1,0,2:T(8,128)S(1)} %copy.262, bf16[1,1,20,20,6,864]{5,1,4,3,2,0:T(2,128)(2,1)} %get-tuple-element.18, f32[6,864,20]{1,0,2:T(8,128)S(1)} %copy.263, ...), kind=kLoop, calls=%fused_computation.59 | loop fusion | flops 20321280 | bytes 10782720 | tf_op jit(solution)/shard_map/bokr,oikr->bikr/dot_general | solution.py:102
  721.0 0.4 copy.146
  721.9 1.0 fusion.76
  723.1 0.6 convolution_bitcast_fusion.2
  724.1 8.4 %all_to_all.44 = f32[4,1,6912]{2,1,0:T(1,128)S(1)} all-to-all(f32[4,1,6912]{2,1,0:T(1,128)S(1)} %reshape.332), channel_id=1, replica_groups=mesh['aa'=8,'ba'=4] {'ba'}, dimensions={0} | all-to-all | bytes 221184 | tf_op jit(solution)/shard_map/all_to_all | solution.py:81
  732.5 0.6 broadcast.116
  733.1 1.0 reduce.19
  734.1 0.5 reshape.333
  734.6 2.2 fusion.75
  736.9 1.2 reshape.334
  738.1 8.1 %all_to_all.45 = bf16[8,2,4608]{2,1,0:T(2,128)(2,1)S(1)} all-to-all(bf16[8,2,4608]{2,1,0:T(2,128)(2,1)S(1)} %reshape.334), channel_id=1, replica_groups=mesh['aa'=8,'ba'=4] {'aa'}, dimensions={0} | all-to-all | bytes 294912 | tf_op jit(solution)/shard_map/all_to_all | solution.py:81
  746.1 1.5 reshape.335
  747.6 3.1 fusion.61
  (47 shorter events, 2.3 us)
Async XLA Ops:
  0.0 15.7 %copy-start.9 = (bf16[2048,2,8,36,1,1]{0,3,2,1,5,4:T(8,128)(2,1)S(1)}, bf16[2048,2,8,36,1,1]{0,3,2,1,5,4:T(8,128)(2,1)}, u32[]{:S(2)}) copy-start(bf16[2048,2,8,36,1,1]{0,3,2,1,5,4:T(8,128)(2,1)} %constant.49) | copy-start | bytes 7077892
  11.8 3.9 copy-start
  76.1 71.8 %copy-start.11 = (bf16[2,8,8,2,4,6,1,1]{2,5,0,1,4,3,7,6:T(8,128)(2,1)S(1)}, bf16[2,8,8,2,4,6,1,1]{2,5,0,1,4,3,7,6:T(8,128)(2,1)}, u32[]{:S(2)}) copy-start(bf16[2,8,8,2,4,6,1,1]{2,5,0,1,4,3,7,6:T(8,128)(2,1)} %constant.50) | copy-start | bytes 36868
  173.3 40.0 %all-to-all-start.1 = ((bf16[4,2,69120]{2,1,0:T(2,128)(2,1)}), bf16[4,2,69120]{2,1,0:T(2,128)(2,1)S(1)}, u32[]{:S(2)}, u32[]{:S(2)}) async-start(bf16[4,2,69120]{2,1,0:T(2,128)(2,1)} %reshape.322), calls=%async_computation.1 | async-start | bytes 2211840 | tf_op jit(solution)/shard_map/all_to_all | solution.py:81
  178.4 46.9 %copy-start.1 = (bf16[2,4,16,2,24,1,1]{4,2,0,1,3,6,5:T(8,128)(2,1)S(1)}, bf16[2,4,16,2,24,1,1]{4,2,0,1,3,6,5:T(8,128)(2,1)}, u32[]{:S(2)}) copy-start(bf16[2,4,16,2,24,1,1]{4,2,0,1,3,6,5:T(8,128)(2,1)} %constant.51) | copy-start | bytes 36868
  236.3 17.7 %copy-start.4 = (bf16[2,24,2,4,16,1,1]{1,4,0,3,2,6,5:T(8,128)(2,1)S(1)}, bf16[2,24,2,4,16,1,1]{1,4,0,3,2,6,5:T(8,128)(2,1)}, u32[]{:S(2)}) copy-start(bf16[2,24,2,4,16,1,1]{1,4,0,3,2,6,5:T(8,128)(2,1)} %constant.52) | copy-start | bytes 36868
  255.3 56.1 %copy-start.13 = (bf16[2,4,6,2,8,8,1,1]{2,5,0,1,4,3,7,6:T(8,128)(2,1)S(1)}, bf16[2,4,6,2,8,8,1,1]{2,5,0,1,4,3,7,6:T(8,128)(2,1)}, u32[]{:S(2)}) copy-start(bf16[2,4,6,2,8,8,1,1]{2,5,0,1,4,3,7,6:T(8,128)(2,1)} %constant.53) | copy-start | bytes 36868
  356.5 39.5 %all-to-all-start.3 = ((bf16[8,2,92160]{2,1,0:T(2,128)(2,1)}), bf16[8,2,92160]{2,1,0:T(2,128)(2,1)S(1)}, u32[]{:S(2)}, u32[]{:S(2)}) async-start(bf16[8,2,92160]{2,1,0:T(2,128)(2,1)} %reshape.326), calls=%async_computation.3 | async-start | bytes 5898240 | tf_op jit(solution)/shard_map/all_to_all | solution.py:81
  360.3 10.2 %copy-start.5 = (bf16[2,20,20]{2,0,1:T(2,128)(2,1)S(1)}, bf16[2,20,20]{2,0,1:T(2,128)(2,1)}, u32[]{:S(2)}) copy-start(bf16[2,20,20]{2,0,1:T(2,128)(2,1)} %param.20) | copy-start | bytes 4804
  360.3 10.3 %copy-start.6 = (f32[20]{0:T(128)S(1)}, f32[20]{0:T(128)}, u32[]{:S(2)}) copy-start(f32[20]{0:T(128)} %param.21) | copy-start | bytes 244
  438.9 52.2 %copy-start.10 = (bf16[2048,2,8,36,1,1]{0,3,2,1,5,4:T(8,128)(2,1)S(1)}, bf16[2048,2,8,36,1,1]{0,3,2,1,5,4:T(8,128)(2,1)}, u32[]{:S(2)}) copy-start(bf16[2048,2,8,36,1,1]{0,3,2,1,5,4:T(8,128)(2,1)} %constant.49) | copy-start | bytes 7077892
  559.9 69.7 %copy-start.12 = (bf16[2,8,8,2,4,6,1,1]{2,5,0,1,4,3,7,6:T(8,128)(2,1)S(1)}, bf16[2,8,8,2,4,6,1,1]{2,5,0,1,4,3,7,6:T(8,128)(2,1)}, u32[]{:S(2)}) copy-start(bf16[2,8,8,2,4,6,1,1]{2,5,0,1,4,3,7,6:T(8,128)(2,1)} %constant.50) | copy-start | bytes 36868
  638.4 57.7 %copy-start.2 = (bf16[2,4,16,2,24,1,1]{4,2,0,1,3,6,5:T(8,128)(2,1)S(1)}, bf16[2,4,16,2,24,1,1]{4,2,0,1,3,6,5:T(8,128)(2,1)}, u32[]{:S(2)}) copy-start(bf16[2,4,16,2,24,1,1]{4,2,0,1,3,6,5:T(8,128)(2,1)} %constant.51) | copy-start | bytes 36868
  707.1 14.8 %copy-start.7 = (f32[20]{0:T(128)S(1)}, f32[20]{0:T(128)}, u32[]{:S(2)}) copy-start(f32[20]{0:T(128)} %param.21) | copy-start | bytes 244
  707.1 15.9 %copy-start.3 = (f32[2,24,2,4,16,1]{1,4,0,5,3,2:T(8,128)S(1)}, f32[2,24,2,4,16,1]{1,4,0,5,3,2:T(8,128)}, u32[]{:S(2)}) copy-start(f32[2,24,2,4,16,1]{1,4,0,5,3,2:T(8,128)} %constant.55) | copy-start | bytes 73732
  720.9 26.8 %copy-start.8 = (bf16[2,8,36,2048,1]{3,2,0,4,1:T(8,128)(2,1)S(1)}, bf16[2,8,36,2048,1]{3,2,0,4,1:T(8,128)(2,1)}, u32[]{:S(2)}) copy-start(bf16[2,8,36,2048,1]{3,2,0,4,1:T(8,128)(2,1)} %constant.57) | copy-start | bytes 7077892
